TPU v7x, 32 devices: a whole 2x2x4 slice. The times are simulated.
32 devices in a mesh: layer: 2 (over x), row: 16 (over z, y, core).
Axes of the slice: x: 2, y: 2, z: 4, core: 2. Of those that a mesh axis runs over, the one named last changes fastest.
Arguments:
- leaf_rhs: float32 [2, 16, 256, 384], P('layer', 'row'), may hold values from -6 to 6
- leaf_inverse: float32 [2, 16, 256, 256], P('layer', 'row'), may hold values from -0.375 to 0.375
- leaf_coupling: float32 [2, 16, 4, 512, 256], P('layer', 'row'), may hold values from -0.09375 to 0.09375
- parent: int32 [2, 16], P('layer', 'row'), may hold values from 0 to 3
- sep_rhs: float32 [2, 4, 512, 384], P('layer', None, 'row'), may hold values from -6 to 6
- sep_inverse: float32 [2, 4, 512, 512], P('layer', None, 'row'), may hold values from -0.25 to 0.25
- sep_coupling: float32 [2, 3, 512, 512], P('layer', None, 'row'), may hold values from -0.125 to 0.125
- root_coupling: float32 [2, 512, 512], P('layer', 'row'), may hold values from -0.1875 to 0.1875
- root_rhs: float32 [512, 384], P('row'), may hold values from -6 to 6
- root_inverse: float32 [512, 512], P('row'), may hold values from -0.25 to 0.25
Outputs:
- sep_solution: float32 [2, 4, 512, 384], P('layer', None, 'row')
- root_solution: float32 [512, 384], P('row')
All inputs are finite; a program needn't handle non-finite values.
Results may differ from a plain program's by a relative error of at most 0.0003.
Values sent between devices are 32-bit elements; how exact they have to be, the bound alone decides.
A program may use at most 64 MiB of HBM per device.

v0:
```python
import functools

import jax
import jax.numpy as jnp
from jax import lax
from jax.experimental import pallas as pl
from jax.experimental.pallas import tpu as pltpu
from jax.sharding import PartitionSpec as P

MESH = pl.DeviceIdType.MESH
NN = (((1,), (0,)), ((), ()))
NT = (((1,), (1,)), ((), ()))
HALVES = 2
LAG = 2


def split(a):
    high = a.astype(jnp.bfloat16)
    return high, (a - high.astype(jnp.float32)).astype(jnp.bfloat16)


def dot3(a, b, dims):
    (ah, al), (bh, bl) = a, b
    dot = functools.partial(lax.dot_general, dimension_numbers=dims, preferred_element_type=jnp.float32)
    return dot(ah, bh) + (dot(ah, bl) + dot(al, bh))


def kernel(
    n_z,
    parent,
    leaf_rhs,
    leaf_inverse,
    leaf_coupling,
    sep_rhs,
    sep_inverse,
    sep_coupling,
    root_coupling,
    root_rhs,
    root_inverse,
    sep_out,
    root_out,
    g_inv,
    g_chain,
    g_rc,
    g_rr,
    g_ri,
    part,
    from_core,
    to_y,
    from_y,
    mine,
    fwd,
    bwd,
    from_left,
    from_right,
    total,
    solved,
    padded,
    turned,
    pieces,
    root_send,
    root_recv,
    root_full,
    w_send,
    w_recv,
    c_send,
    c_recv,
    y_send,
    y_recv,
    f_send,
    f_recv,
    b_send,
    b_recv,
    a_send,
    a_recv,
    o_send,
    o_recv,
    x_send,
    x_recv,
):
    seps, rows, right = sep_rhs.shape
    width = sep_inverse.shape[2]
    zrows = width // n_z
    half, quarter = right // 2, right // 4
    sub = quarter // HALVES

    layer = lax.axis_index("layer")
    me = lax.axis_index("row")
    z, y, c = me // 4, (me // 2) % 2, me % 2
    plane = 2 * y + c
    base = 4 * z

    def at(zz, yy, cc):
        return (layer, 4 * zz + 2 * yy + cc)

    core_peer = at(z, y, 1 - c)
    y_peer = at(z, 1 - y, c)
    far_peer = at(z, 1 - y, 1 - c)
    x_peer = (1 - layer, me)
    left, right_peer = (layer, me - 4), (layer, me + 4)
    z_peers = [at((z + d) % n_z, y, c) for d in range(1, n_z)]
    plane_peers = [core_peer, y_peer, far_peer]

    def remote(src, dst, send, recv, peer):
        return pltpu.make_async_remote_copy(
            src_ref=src, dst_ref=dst, send_sem=send, recv_sem=recv, device_id=peer, device_id_type=MESH
        )

    barrier = pltpu.get_barrier_semaphore()
    peers = plane_peers + z_peers + [x_peer]
    for peer in peers:
        pl.semaphore_signal(barrier, inc=1, device_id=peer, device_id_type=MESH)
    pl.semaphore_wait(barrier, len(peers))

    own_rows = pl.ds(pl.multiple_of(plane * rows, rows), rows)
    y_rows = pl.ds(pl.multiple_of((2 * (1 - y) + c) * rows, rows), rows)
    weights = [
        (sep_inverse, g_inv, True),
        (sep_coupling, g_chain, True),
        (root_coupling, g_rc, False),
        (root_rhs, g_rr, False),
        (root_inverse, g_ri, False),
    ]

    def slot(ref, deep, where):
        return ref.at[:, where, :] if deep else ref.at[where, :]

    def weight(way, n):
        source, dest, deep = weights[n]
        if way == 2:
            source, where = slot(dest, deep, y_rows), y_rows
        else:
            where = own_rows
        return remote(
            source,
            slot(dest, deep, where),
            w_send.at[way, n],
            w_recv.at[way, n],
            y_peer if way == 0 else core_peer,
        )

    def weight_start(way, which):
        for n in which:
            weight(way, n).start()

    weight_start(0, (0,))
    g_inv[:, own_rows, :] = sep_inverse[...]
    g_chain[:, own_rows, :] = sep_coupling[...]
    g_rc[own_rows, :] = root_coupling[...]
    g_rr[own_rows, :] = root_rhs[...]
    g_ri[own_rows, :] = root_inverse[...]

    leaf = dot3(split(leaf_inverse[...]), split(leaf_rhs[...]), NN)
    leaf_t = split(leaf.T)
    zlanes = pl.ds(pl.multiple_of(z * zrows, 128), zrows)
    core_cols = pl.ds(pl.multiple_of(half * c, 8), half)
    other_core_cols = pl.ds(pl.multiple_of(half * (1 - c), 8), half)
    padded[...] = jnp.zeros_like(padded)

    def core_copy(k):
        return remote(
            part.at[k, other_core_cols, :], from_core.at[k], c_send.at[k], c_recv.at[k], core_peer
        )

    def stage_a(k):
        keep = jnp.where(parent[0, 0] <= k, -1.0, 0.0).astype(jnp.float32)
        part[k] = dot3(leaf_t, split(leaf_coupling[k]), NT) * keep
        padded[own_rows, :] = sep_rhs[k]
        part[k, :, zlanes] += padded[...].T
        core_copy(k).start()

    own_y = pl.multiple_of(quarter * y, 8)
    peer_y = pl.multiple_of(quarter * (1 - y), 8)

    def y_copy(k, h):
        where = pl.ds(h * sub, sub)
        return remote(
            to_y.at[k, where, :], from_y.at[k, where, :], y_send.at[k, h], y_recv.at[k, h], y_peer
        )

    def stage_b(k):
        core_copy(k).wait_recv()
        to_y[k] = (
            part[k, pl.ds(pl.multiple_of(half * c + peer_y, 8), quarter), :]
            + from_core[k, pl.ds(peer_y, quarter), :]
        )
        for h in range(HALVES):
            y_copy(k, h).start()

    def fwd_copy(k, h):
        where = pl.ds(h * sub, sub)
        return remote(
            fwd.at[k, where, :], from_left.at[k, where, :], f_send.at[k, h], f_recv.at[k, h], right_peer
        )

    def bwd_copy(k, h):
        where = pl.ds(h * sub, sub)
        return remote(
            bwd.at[k, where, :], from_right.at[k, where, :], b_send.at[k, h], b_recv.at[k, h], left
        )

    def stage_c(k, h):
        where = pl.ds(h * sub, sub)
        y_copy(k, h).wait_recv()
        mine[k, where, :] = (
            part[k, pl.ds(pl.multiple_of(half * c + own_y + h * sub, 8), sub), :]
            + from_core[k, pl.ds(pl.multiple_of(own_y + h * sub, 8), sub), :]
            + from_y[k, where, :]
        )

    def hop(k, h, number):
        where = pl.ds(h * sub, sub)

        @pl.when(z == number)
        def _():
            if number == 0:
                fwd[k, where, :] = mine[k, where, :]
            else:
                fwd_copy(k, h).wait_recv()
                fwd[k, where, :] = mine[k, where, :] + from_left[k, where, :]
            fwd_copy(k, h).start()

        @pl.when(z == n_z - 1 - number)
        def _():
            if number == 0:
                bwd[k, where, :] = mine[k, where, :]
            else:
                bwd_copy(k, h).wait_recv()
                bwd[k, where, :] = mine[k, where, :] + from_right[k, where, :]
            bwd_copy(k, h).start()

    def finish(k, h):
        where = pl.ds(h * sub, sub)

        @pl.when(z == 0)
        def _():
            bwd_copy(k, h).wait_recv()
            total[k, where, :] = mine[k, where, :] + from_right[k, where, :]

        @pl.when(z == n_z - 1)
        def _():
            fwd_copy(k, h).wait_recv()
            total[k, where, :] = mine[k, where, :] + from_left[k, where, :]

        @pl.when(jnp.logical_and(z > 0, z < n_z - 1))
        def _():
            total[k, where, :] = mine[k, where, :] + (from_left[k, where, :] + from_right[k, where, :])

    def z_lanes(zz):
        return pl.ds(pl.multiple_of(zz * zrows, 128), zrows)

    def along_z(ref, k, d, sender):
        where = z_lanes((z - d + n_z) % n_z if sender else z)
        return remote(
            ref.at[:, where], ref.at[:, where], a_send.at[k, d - 1], a_recv.at[k, d - 1], z_peers[d - 1]
        )

    def out_copy(k, n):
        peer_plane = (2 * y + 1 - c, 2 * (1 - y) + c, 2 * (1 - y) + 1 - c)[n]
        rows_there = pl.ds(pl.multiple_of(peer_plane * rows, rows), rows)
        return remote(
            turned.at[k, rows_there, :], pieces.at[k, n], o_send.at[k, n], o_recv.at[k, n], plane_peers[n]
        )

    def turn(k, value):
        turned[k, :, pl.ds(0, quarter)] = value.T
        for n in range(3):
            out_copy(k, n).start()

    def assemble(k):
        for n in range(3):
            out_copy(k, n).wait_recv()
        own = turned[k, own_rows, :][:, :quarter]
        by_core, by_y, by_far = (pieces[k, n][:, :quarter] for n in range(3))
        low_y, low_core = y == 0, c == 0
        same = (jnp.where(low_y, own, by_y), jnp.where(low_y, by_y, own))
        other = (jnp.where(low_y, by_core, by_far), jnp.where(low_y, by_far, by_core))
        blocks = [jnp.where(low_core, same[n], other[n]) for n in range(2)]
        blocks += [jnp.where(low_core, other[n], same[n]) for n in range(2)]
        return jnp.concatenate(blocks, axis=1)

    def wait_along_z(ref, k):
        for d in range(1, n_z):
            along_z(ref, k, d, True).wait_recv()

    def chain(k):
        value = dot3(split(total[k]), split(g_inv[k]), NT)
        if k > 0:
            wait_along_z(solved.at[k - 1], k - 1)
            value = value - dot3(split(solved[k - 1]), split(g_chain[k - 1]), NT)
        solved[k, :, zlanes] = value
        for d in range(1, n_z):
            along_z(solved.at[k], k, d, False).start()
        turn(k, value)

    stage_a(0)
    weight_start(1, (0,))
    stage_a(1)
    stage_b(0)
    chunks = [(k, h) for k in range(seps) for h in range(HALVES)]

    def ahead(step):
        k = step // HALVES + 2
        if step % HALVES == 0 and k < seps:
            stage_a(k)
            stage_b(k - 1)
        if step == HALVES * (seps - 2):
            stage_b(seps - 1)
            weight_start(1, (1, 2, 3, 4))
            weight_start(0, (1, 2, 3, 4))
            for n in (0,):
                weight(0, n).wait_recv()
                weight(2, n).start()

    for step in range(len(chunks) + LAG * (n_z - 1) + 1):
        ahead(step)
        for number in reversed(range(n_z - 1)):
            j = step - LAG * number
            if 0 <= j < len(chunks):
                if number == 0:
                    stage_c(*chunks[j])
                hop(*chunks[j], number)
        j = step - LAG * (n_z - 1)
        if 0 <= j < len(chunks):
            k, h = chunks[j]
            finish(k, h)
            if h == HALVES - 1:
                if k == 0:
                    weight(0, 1).wait_recv()
                    weight(2, 1).start()
                if k < 2:
                    for way in (1, 2):
                        weight(way, k).wait_recv()
                if k == seps - 1:
                    for n in range(2, 5):
                        weight(0, n).wait_recv()
                        weight(2, n).start()
                chain(k)

    last = seps - 1
    for n in range(2, 5):
        for way in (1, 2):
            weight(way, n).wait_recv()
    root_rhs_t = g_rr[...].T
    turned_rr = part.at[0, :, pl.ds(0, zrows)]
    for k in range(seps):
        core_copy(k).wait_send()
    turned_rr[...] = root_rhs_t
    my_cols = pl.ds(pl.multiple_of(half * c + quarter * y, 8), quarter)
    wait_along_z(solved.at[last], last)
    term = dot3(split(solved[last]), split(g_rc[...]), NT)
    root_send[...] = term
    swap = remote(root_send, root_recv, x_send.at[0], x_recv.at[0], x_peer)
    swap.start()
    for k in range(seps):
        sep_out[k] = assemble(k)
    swap.wait_recv()
    root_full[:, zlanes] = part[0, my_cols, pl.ds(0, zrows)] - (term + root_recv[...])
    for d in range(1, n_z):
        along_z(root_full, seps, d, False).start()
    wait_along_z(root_full, seps)
    turn(seps, dot3(split(root_full[...]), split(g_ri[...]), NT))
    root_out[...] = assemble(seps)

    for way in range(3):
        for n in range(5):
            weight(way, n).wait_send()
    for k, h in chunks:
        y_copy(k, h).wait_send()

        @pl.when(z < n_z - 1)
        def _():
            fwd_copy(k, h).wait_send()

        @pl.when(z > 0)
        def _():
            bwd_copy(k, h).wait_send()

    for k in range(seps + 1):
        ref = solved.at[k] if k < seps else root_full
        for d in range(1, n_z):
            along_z(ref, k, d, False).wait_send()
        for n in range(3):
            out_copy(k, n).wait_send()
    swap.wait_send()


def fused(
    n_z,
    leaf_rhs,
    leaf_inverse,
    leaf_coupling,
    parent,
    sep_rhs,
    sep_inverse,
    sep_coupling,
    root_coupling,
    root_rhs,
    root_inverse,
):
    seps, rows, right = sep_rhs.shape[1:]
    width = sep_inverse.shape[3]
    zrows, half, quarter = width // n_z, right // 2, right // 4
    f32 = jnp.float32
    dma = pltpu.SemaphoreType.DMA
    vmem = pl.BlockSpec(memory_space=pltpu.VMEM)
    scratch = [
        (seps, zrows, width),
        (seps - 1, zrows, width),
        (zrows, width),
        (zrows, right),
        (zrows, width),
        (seps, right, width),
        (seps, half, width),
    ]
    scratch += [(seps, quarter, width)] * 9
    scratch += [
        (zrows, right),
        (seps + 1, zrows, 128),
        (seps + 1, 3, rows, 128),
        (quarter, zrows),
        (quarter, zrows),
        (quarter, width),
    ]
    sems = [(3, 5)] * 2 + [(seps,)] * 2 + [(seps, HALVES)] * 6
    sems += [(seps + 1, n_z - 1)] * 2 + [(seps + 1, 3)] * 2 + [(1,)] * 2
    sep, root = pl.pallas_call(
        functools.partial(kernel, n_z),
        out_shape=(
            jax.ShapeDtypeStruct((seps, rows, right), f32),
            jax.ShapeDtypeStruct((rows, right), f32),
        ),
        in_specs=[pl.BlockSpec(memory_space=pltpu.SMEM)] + [vmem] * 9,
        out_specs=(vmem, vmem),
        scratch_shapes=[pltpu.VMEM(s, f32) for s in scratch] + [dma(s) for s in sems],
        compiler_params=pltpu.CompilerParams(
            collective_id=0, has_side_effects=True, vmem_limit_bytes=60 * 2**20
        ),
        name="forward_solve",
    )(
        parent,
        leaf_rhs.reshape(leaf_rhs.shape[2:]),
        leaf_inverse.reshape(leaf_inverse.shape[2:]),
        leaf_coupling.reshape(leaf_coupling.shape[2:]),
        sep_rhs.reshape(sep_rhs.shape[1:]),
        sep_inverse.reshape(sep_inverse.shape[1:]),
        sep_coupling.reshape(sep_coupling.shape[1:]),
        root_coupling.reshape(root_coupling.shape[1:]),
        root_rhs,
        root_inverse,
    )
    return sep[None], root


def body(
    leaf_rhs,
    leaf_inverse,
    leaf_coupling,
    parent,
    sep_rhs,
    sep_inverse,
    sep_coupling,
    root_coupling,
    root_rhs,
    root_inverse,
):
    highest = lax.Precision.HIGHEST
    sep_count = sep_rhs.shape[1]
    row_count = sep_rhs.shape[2]
    row_start = lax.axis_index("row") * row_count
    leaf_solution = jnp.dot(leaf_inverse[0, 0], leaf_rhs[0, 0], precision=highest)
    levels = jnp.arange(sep_count, dtype=jnp.int32)
    keep_mask = (levels >= parent[0, 0]).astype(jnp.float32)

    def residual_term(k):
        coupled = jnp.dot(leaf_coupling[0, 0, k], leaf_solution, precision=highest) * keep_mask[k]
        own_rhs = lax.dynamic_update_slice_in_dim(
            jnp.zeros_like(coupled), sep_rhs[0, k], row_start, 0
        )
        return own_rhs - coupled

    residual_list = [lax.psum(residual_term(k), "row") for k in range(sep_count)]
    local_rows = [
        jnp.dot(sep_inverse[0, k], residual_list[k], precision=highest) for k in range(sep_count)
    ]
    solved = []
    gathered = None
    for k in range(sep_count):
        current = local_rows[k]
        if k > 0:
            current = current - jnp.dot(sep_coupling[0, k - 1], gathered, precision=highest)
        solved.append(current)
        gathered = lax.all_gather(current, "row", axis=0, tiled=True)
    sep_out = jnp.stack(solved)[None]
    root_term = jnp.dot(root_coupling[0], gathered, precision=highest)
    root_sum = lax.psum(root_term, "layer")
    root_residual = root_rhs - root_sum
    root_out = jnp.dot(
        root_inverse, lax.all_gather(root_residual, "row", axis=0, tiled=True), precision=highest
    )
    return (sep_out, root_out)


def solution(mesh):
    n_layer, n_row = mesh.shape["layer"], mesh.shape["row"]

    def per_device(*arrays):
        right, width = arrays[0].shape[3], arrays[5].shape[3]
        n_z = n_row // 4
        fits = (
            n_layer == 2
            and n_row in (8, 16)
            and width % (128 * n_z) == 0
            and right % (32 * HALVES) == 0
            and right // 4 <= 128
            and arrays[4].shape[1] >= 3
        )
        return functools.partial(fused, n_z)(*arrays) if fits else body(*arrays)

    return jax.shard_map(
        per_device,
        mesh=mesh,
        in_specs=(
            P("layer", "row", None, None),
            P("layer", "row", None, None),
            P("layer", "row", None, None, None),
            P("layer", "row"),
            P("layer", None, "row", None),
            P("layer", None, "row", None),
            P("layer", None, "row", None),
            P("layer", "row", None),
            P("row", None),
            P("row", None),
        ),
        out_specs=(P("layer", None, "row", None), P("row", None)),
        check_vma=False,
    )
```

profile of v0, /device:TPU:0, one launch (start us, length us, event | category | flops | bytes accessed | tf_op | source)
XLA Modules:
  0.0 80.2 jit_solution(178943416519764104)
XLA Ops:
  1.3 75.9 %forward_solve.1 = (f32[4,32,384]{2,1,0:T(8,128)}, f32[32,384]{1,0:T(8,128)}) custom-call(s32[1,1]{1,0:T(1,128)S(6)} %copy.14.parent, f32[256,384]{1,0:T(8,128)} %bitcast.9, f32[256,256]{1,0:T(8,128)} %bitcast.10, f32[4,512,256]{2,1,0:T(8,128)} %bitcast.8, f32[4,32,384]{2,1,0:T(8,128)} %bitcast.13, f32[4,32,512]{2,1,0:T(8,128)} %bitcast.11, ...), custom_call_target="tpu_custom_call" | custom-call | tf_op jit(solution)/shard_map/forward_solve/pallas_call | solution.py:427
  77.2 1.6 %copy.15 = f32[1,4,32,384]{3,2,1,0:T(8,128)} copy(f32[1,4,32,384]{3,2,1,0:T(8,128)} %bitcast.12) | data formatting | bytes 393216
  78.8 1.4 %copy.16 = f32[32,384]{1,0:T(8,128)} copy(f32[32,384]{1,0:T(8,128)} %get-tuple-element.9) | data formatting | bytes 98304
where the time goes:
time: 80.4 us; the launch traced here: 80.2 us
  Pallas kernels  75.9 us (94%)
  local copies, waits for them, and re-layouts  3.04 us (4%)
  between operations  1.29 us (2%)
    pallas_call x1, Pallas kernels, fused(): pl.pallas_call(functools.partial(kernel, n_z), out_shape=(jax.ShapeDtypeS...  75.9 us
    unnamed x2, local copies, waits for them, and re-layouts  3.04 us

commit v1 on v0

--- a/solution.py
+++ b/solution.py
@@ -12,6 +12,8 @@
 NT = (((1,), (1,)), ((), ()))
 HALVES = 2
 LAG = 2
+BEFORE = 1
+SHIFT = (0, 0, 0, 0)
 
 
 def split(a):
@@ -39,6 +41,10 @@
     root_inverse,
     sep_out,
     root_out,
+    v_rhs,
+    v_inv,
+    v_coup,
+    v_sep,
     g_inv,
     g_chain,
     g_rc,
@@ -61,6 +67,8 @@
     root_send,
     root_recv,
     root_full,
+    load,
+    own_load,
     w_send,
     w_recv,
     c_send,
@@ -78,17 +86,17 @@
     x_send,
     x_recv,
 ):
-    seps, rows, right = sep_rhs.shape
-    width = sep_inverse.shape[2]
+    seps, rows, right = v_sep.shape
+    width = v_coup.shape[1]
     zrows = width // n_z
     half, quarter = right // 2, right // 4
     sub = quarter // HALVES
+    last = seps - 1
 
     layer = lax.axis_index("layer")
     me = lax.axis_index("row")
     z, y, c = me // 4, (me // 2) % 2, me % 2
     plane = 2 * y + c
-    base = 4 * z
 
     def at(zz, yy, cc):
         return (layer, 4 * zz + 2 * yy + cc)
@@ -110,67 +118,86 @@
     peers = plane_peers + z_peers + [x_peer]
     for peer in peers:
         pl.semaphore_signal(barrier, inc=1, device_id=peer, device_id_type=MESH)
-    pl.semaphore_wait(barrier, len(peers))
 
     own_rows = pl.ds(pl.multiple_of(plane * rows, rows), rows)
     y_rows = pl.ds(pl.multiple_of((2 * (1 - y) + c) * rows, rows), rows)
-    weights = [
-        (sep_inverse, g_inv, True),
-        (sep_coupling, g_chain, True),
-        (root_coupling, g_rc, False),
-        (root_rhs, g_rr, False),
-        (root_inverse, g_ri, False),
+    weights = [(sep_inverse.at[k], g_inv.at[k]) for k in range(seps)]
+    weights += [(sep_coupling.at[k], g_chain.at[k]) for k in range(last)]
+    weights += [(root_coupling, g_rc), (root_rhs, g_rr), (root_inverse, g_ri)]
+    inv_at, chain_at, rc_at, rr_at, ri_at = 0, seps, seps + last, seps + last + 1, seps + last + 2
+
+    loads = [
+        pltpu.make_async_copy(leaf_inverse, v_inv, load.at[0]),
+        pltpu.make_async_copy(leaf_rhs, v_rhs, load.at[1]),
+        pltpu.make_async_copy(sep_rhs, v_sep, load.at[2]),
     ]
-
-    def slot(ref, deep, where):
-        return ref.at[:, where, :] if deep else ref.at[where, :]
+    loads += [pltpu.make_async_copy(leaf_coupling.at[k], v_coup.at[k], load.at[3 + k]) for k in range(seps)]
+    for n in (0, 1, 3, 2) + tuple(range(4, 3 + seps)):
+        loads[n].start()
+    own_loads = [
+        pltpu.make_async_copy(source, dest.at[own_rows, :], own_load.at[n])
+        for n, (source, dest) in enumerate(weights)
+    ]
+    for copy in own_loads:
+        copy.start()
 
     def weight(way, n):
-        source, dest, deep = weights[n]
+        source, dest = weights[n]
         if way == 2:
-            source, where = slot(dest, deep, y_rows), y_rows
+            source, where = dest.at[y_rows, :], y_rows
         else:
             where = own_rows
         return remote(
             source,
-            slot(dest, deep, where),
+            dest.at[where, :],
             w_send.at[way, n],
             w_recv.at[way, n],
             y_peer if way == 0 else core_peer,
         )
 
-    def weight_start(way, which):
-        for n in which:
-            weight(way, n).start()
-
-    weight_start(0, (0,))
-    g_inv[:, own_rows, :] = sep_inverse[...]
-    g_chain[:, own_rows, :] = sep_coupling[...]
-    g_rc[own_rows, :] = root_coupling[...]
-    g_rr[own_rows, :] = root_rhs[...]
-    g_ri[own_rows, :] = root_inverse[...]
-
-    leaf = dot3(split(leaf_inverse[...]), split(leaf_rhs[...]), NN)
+    def relay(n):
+        weight(0, n).wait_recv()
+        weight(2, n).start()
+
+    def weight_ready(n):
+        own_loads[n].wait()
+        weight(1, n).wait_recv()
+        weight(2, n).wait_recv()
+
+    zlanes = pl.ds(pl.multiple_of(z * zrows, 128), zrows)
+    own_y = pl.multiple_of(quarter * y, 8)
+    peer_y = pl.multiple_of(quarter * (1 - y), 8)
+    padded[...] = jnp.zeros_like(padded)
+
+    def core_copy(k, q):
+        there = (peer_y, own_y)[q]
+        return remote(
+            part.at[k, pl.ds(pl.multiple_of(half * (1 - c) + there, 8), quarter), :],
+            from_core.at[k, pl.ds(there, quarter), :],
+            c_send.at[k, q],
+            c_recv.at[k, q],
+            core_peer,
+        )
+
+    loads[0].wait()
+    loads[1].wait()
+    leaf = dot3(split(v_inv[...]), split(v_rhs[...]), NN)
     leaf_t = split(leaf.T)
-    zlanes = pl.ds(pl.multiple_of(z * zrows, 128), zrows)
-    core_cols = pl.ds(pl.multiple_of(half * c, 8), half)
-    other_core_cols = pl.ds(pl.multiple_of(half * (1 - c), 8), half)
-    padded[...] = jnp.zeros_like(padded)
-
-    def core_copy(k):
-        return remote(
-            part.at[k, other_core_cols, :], from_core.at[k], c_send.at[k], c_recv.at[k], core_peer
-        )
 
     def stage_a(k):
         keep = jnp.where(parent[0, 0] <= k, -1.0, 0.0).astype(jnp.float32)
-        part[k] = dot3(leaf_t, split(leaf_coupling[k]), NT) * keep
-        padded[own_rows, :] = sep_rhs[k]
+        loads[3 + k].wait()
+        part[k] = dot3(leaf_t, split(v_coup[k]), NT) * keep
+        if k == 0:
+            loads[2].wait()
+        padded[own_rows, :] = v_sep[k]
         part[k, :, zlanes] += padded[...].T
-        core_copy(k).start()
-
-    own_y = pl.multiple_of(quarter * y, 8)
-    peer_y = pl.multiple_of(quarter * (1 - y), 8)
+        if k == 0:
+            pl.semaphore_wait(barrier, len(peers))
+            for n in range(BEFORE):
+                weight(0, n).start()
+        for q in range(2):
+            core_copy(k, q).start()
 
     def y_copy(k, h):
         where = pl.ds(h * sub, sub)
@@ -179,7 +206,7 @@
         )
 
     def stage_b(k):
-        core_copy(k).wait_recv()
+        core_copy(k, 0).wait_recv()
         to_y[k] = (
             part[k, pl.ds(pl.multiple_of(half * c + peer_y, 8), quarter), :]
             + from_core[k, pl.ds(peer_y, quarter), :]
@@ -201,6 +228,8 @@
 
     def stage_c(k, h):
         where = pl.ds(h * sub, sub)
+        if h == 0:
+            core_copy(k, 1).wait_recv()
         y_copy(k, h).wait_recv()
         mine[k, where, :] = (
             part[k, pl.ds(pl.multiple_of(half * c + own_y + h * sub, 8), sub), :]
@@ -249,11 +278,10 @@
     def z_lanes(zz):
         return pl.ds(pl.multiple_of(zz * zrows, 128), zrows)
 
-    def along_z(ref, k, d, sender):
+    def along_z(ref, k, h, d, sender):
         where = z_lanes((z - d + n_z) % n_z if sender else z)
-        return remote(
-            ref.at[:, where], ref.at[:, where], a_send.at[k, d - 1], a_recv.at[k, d - 1], z_peers[d - 1]
-        )
+        block = ref.at[pl.ds(h * sub, sub), where]
+        return remote(block, block, a_send.at[k, h, d - 1], a_recv.at[k, h, d - 1], z_peers[d - 1])
 
     def out_copy(k, n):
         peer_plane = (2 * y + 1 - c, 2 * (1 - y) + c, 2 * (1 - y) + 1 - c)[n]
@@ -279,41 +307,57 @@
         blocks += [jnp.where(low_core, other[n], same[n]) for n in range(2)]
         return jnp.concatenate(blocks, axis=1)
 
-    def wait_along_z(ref, k):
+    def wait_along_z(ref, k, h):
         for d in range(1, n_z):
-            along_z(ref, k, d, True).wait_recv()
-
-    def chain(k):
-        value = dot3(split(total[k]), split(g_inv[k]), NT)
+            along_z(ref, k, h, d, True).wait_recv()
+
+    def send_along_z(ref, k, h):
+        for d in range(1, n_z):
+            along_z(ref, k, h, d, False).start()
+
+    def chain(k, h):
+        where = pl.ds(h * sub, sub)
+        if h == 0:
+            weight_ready(inv_at + k)
+            if k > 0:
+                weight_ready(chain_at + k - 1)
+        value = dot3(split(total[k, where, :]), split(g_inv[k]), NT)
         if k > 0:
-            wait_along_z(solved.at[k - 1], k - 1)
-            value = value - dot3(split(solved[k - 1]), split(g_chain[k - 1]), NT)
-        solved[k, :, zlanes] = value
-        for d in range(1, n_z):
-            along_z(solved.at[k], k, d, False).start()
-        turn(k, value)
+            wait_along_z(solved.at[k - 1], k - 1, h)
+            value = value - dot3(split(solved[k - 1, where, :]), split(g_chain[k - 1]), NT)
+        solved[k, where, zlanes] = value
+        send_along_z(solved.at[k], k, h)
+        if h == HALVES - 1:
+            turn(k, solved[k, :, zlanes])
 
     stage_a(0)
-    weight_start(1, (0,))
     stage_a(1)
     stage_b(0)
+    for k in range(2, seps):
+        stage_a(k)
+        stage_b(k - 1)
+    stage_b(last)
+    order = [inv_at, inv_at + 1]
+    for k in range(1, seps):
+        order += [chain_at + k - 1] + [inv_at + k + 1] * (k < last)
+    order += [rc_at, rr_at, ri_at]
+    for n in order:
+        if n >= BEFORE:
+            weight(0, n).start()
+    for n in order:
+        weight(1, n).start()
     chunks = [(k, h) for k in range(seps) for h in range(HALVES)]
-
-    def ahead(step):
-        k = step // HALVES + 2
-        if step % HALVES == 0 and k < seps:
-            stage_a(k)
-            stage_b(k - 1)
-        if step == HALVES * (seps - 2):
-            stage_b(seps - 1)
-            weight_start(1, (1, 2, 3, 4))
-            weight_start(0, (1, 2, 3, 4))
-            for n in (0,):
-                weight(0, n).wait_recv()
-                weight(2, n).start()
-
-    for step in range(len(chunks) + LAG * (n_z - 1) + 1):
-        ahead(step)
+    end = len(chunks) + LAG * (n_z - 1)
+    relays = {}
+    for i, n in enumerate(order):
+        relays.setdefault(2 if n < BEFORE else len(chunks) - 1 + (2 * (i + 1 - BEFORE) * HALVES) // 6, []).append(n)
+    chains = {}
+    for j, (k, h) in enumerate(chunks):
+        chains.setdefault(j + LAG * (n_z - 1) + SHIFT[min(k, 3)], []).append((k, h))
+
+    for step in range(max(end, max(chains) + 1)):
+        for n in relays.pop(step, []):
+            relay(n)
         for number in reversed(range(n_z - 1)):
             j = step - LAG * number
             if 0 <= j < len(chunks):
@@ -322,48 +366,47 @@
                 hop(*chunks[j], number)
         j = step - LAG * (n_z - 1)
         if 0 <= j < len(chunks):
-            k, h = chunks[j]
-            finish(k, h)
-            if h == HALVES - 1:
-                if k == 0:
-                    weight(0, 1).wait_recv()
-                    weight(2, 1).start()
-                if k < 2:
-                    for way in (1, 2):
-                        weight(way, k).wait_recv()
-                if k == seps - 1:
-                    for n in range(2, 5):
-                        weight(0, n).wait_recv()
-                        weight(2, n).start()
-                chain(k)
-
-    last = seps - 1
-    for n in range(2, 5):
-        for way in (1, 2):
-            weight(way, n).wait_recv()
+            finish(*chunks[j])
+        for k, h in chains.get(step, []):
+            chain(k, h)
+    for step in sorted(relays):
+        for n in relays[step]:
+            relay(n)
+
+    for n in range(rc_at, ri_at + 1):
+        weight_ready(n)
     root_rhs_t = g_rr[...].T
     turned_rr = part.at[0, :, pl.ds(0, zrows)]
     for k in range(seps):
-        core_copy(k).wait_send()
+        for q in range(2):
+            core_copy(k, q).wait_send()
     turned_rr[...] = root_rhs_t
-    my_cols = pl.ds(pl.multiple_of(half * c + quarter * y, 8), quarter)
-    wait_along_z(solved.at[last], last)
-    term = dot3(split(solved[last]), split(g_rc[...]), NT)
-    root_send[...] = term
-    swap = remote(root_send, root_recv, x_send.at[0], x_recv.at[0], x_peer)
-    swap.start()
-    for k in range(seps):
+
+    def swap(h):
+        where = pl.ds(h * sub, sub)
+        return remote(root_send.at[where, :], root_recv.at[where, :], x_send.at[h], x_recv.at[h], x_peer)
+
+    for h in range(HALVES):
+        where = pl.ds(h * sub, sub)
+        wait_along_z(solved.at[last], last, h)
+        root_send[where, :] = dot3(split(solved[last, where, :]), split(g_rc[...]), NT)
+        swap(h).start()
+    for k in range(last):
         sep_out[k] = assemble(k)
-    swap.wait_recv()
-    root_full[:, zlanes] = part[0, my_cols, pl.ds(0, zrows)] - (term + root_recv[...])
-    for d in range(1, n_z):
-        along_z(root_full, seps, d, False).start()
-    wait_along_z(root_full, seps)
+    for h in range(HALVES):
+        where = pl.ds(h * sub, sub)
+        swap(h).wait_recv()
+        my_cols = pl.ds(pl.multiple_of(half * c + quarter * y + h * sub, 8), sub)
+        root_full[where, zlanes] = part[0, my_cols, pl.ds(0, zrows)] - (root_send[where, :] + root_recv[where, :])
+        send_along_z(root_full, seps, h)
+    sep_out[last] = assemble(last)
+    for h in range(HALVES):
+        wait_along_z(root_full, seps, h)
     turn(seps, dot3(split(root_full[...]), split(g_ri[...]), NT))
     root_out[...] = assemble(seps)
 
     for way in range(3):
-        for n in range(5):
+        for n in range(len(weights)):
             weight(way, n).wait_send()
     for k, h in chunks:
         y_copy(k, h).wait_send()
@@ -378,11 +421,13 @@
 
     for k in range(seps + 1):
         ref = solved.at[k] if k < seps else root_full
-        for d in range(1, n_z):
-            along_z(ref, k, d, False).wait_send()
+        for h in range(HALVES):
+            for d in range(1, n_z):
+                along_z(ref, k, h, d, False).wait_send()
         for n in range(3):
             out_copy(k, n).wait_send()
-    swap.wait_send()
+    for h in range(HALVES):
+        swap(h).wait_send()
 
 
 def fused(
@@ -400,11 +445,17 @@
 ):
     seps, rows, right = sep_rhs.shape[1:]
     width = sep_inverse.shape[3]
+    deep = leaf_inverse.shape[3]
     zrows, half, quarter = width // n_z, right // 2, right // 4
     f32 = jnp.float32
     dma = pltpu.SemaphoreType.DMA
     vmem = pl.BlockSpec(memory_space=pltpu.VMEM)
+    hbm = pl.BlockSpec(memory_space=pl.ANY)
     scratch = [
+        (deep, right),
+        (deep, deep),
+        (seps, width, deep),
+        (seps, rows, right),
         (seps, zrows, width),
         (seps - 1, zrows, width),
         (zrows, width),
@@ -422,15 +473,17 @@
         (quarter, zrows),
         (quarter, width),
     ]
-    sems = [(3, 5)] * 2 + [(seps,)] * 2 + [(seps, HALVES)] * 6
-    sems += [(seps + 1, n_z - 1)] * 2 + [(seps + 1, 3)] * 2 + [(1,)] * 2
+    n_w = 2 * seps + 2
+    sems = [(3 + seps,), (n_w,)]
+    sems += [(3, n_w)] * 2 + [(seps, 2)] * 2 + [(seps, HALVES)] * 6
+    sems += [(seps + 1, HALVES, n_z - 1)] * 2 + [(seps + 1, 3)] * 2 + [(HALVES,)] * 2
     sep, root = pl.pallas_call(
         functools.partial(kernel, n_z),
         out_shape=(
             jax.ShapeDtypeStruct((seps, rows, right), f32),
             jax.ShapeDtypeStruct((rows, right), f32),
         ),
-        in_specs=[pl.BlockSpec(memory_space=pltpu.SMEM)] + [vmem] * 9,
+        in_specs=[pl.BlockSpec(memory_space=pltpu.SMEM)] + [hbm] * 9,
         out_specs=(vmem, vmem),
         scratch_shapes=[pltpu.VMEM(s, f32) for s in scratch] + [dma(s) for s in sems],
         compiler_params=pltpu.CompilerParams(

time: 80.4 us -> 71.8 us (0.89)
  Pallas kernels: 75.9 us -> 67.3 us
    pallas_call x1, Pallas kernels: 75.9 us -> 67.3 us  [fused(): pl.pallas_call(functools.partial(kernel, n_z), out_shape=(jax.ShapeDtypeS...]
where the time goes in v1:
time: 71.8 us; the launch traced here: 71.6 us
  Pallas kernels  67.3 us (94%)
  local copies, waits for them, and re-layouts  3.04 us (4%)
  between operations  1.29 us (2%)
    pallas_call x1, Pallas kernels, fused(): pl.pallas_call(functools.partial(kernel, n_z), out_shape=(jax.ShapeDtypeS...  67.3 us
    unnamed x2, local copies, waits for them, and re-layouts  3.04 us

profile of v1, /device:TPU:0, one launch (start us, length us, event | category | flops | bytes accessed | tf_op | source)
XLA Modules:
  0.0 71.6 jit_solution(5764730055708263501)
XLA Ops:
  1.3 67.3 %forward_solve.1 = (f32[4,32,384]{2,1,0:T(8,128)}, f32[32,384]{1,0:T(8,128)}) custom-call(s32[1,1]{1,0:T(1,128)S(6)} %copy.14.parent, f32[256,384]{1,0:T(8,128)} %bitcast.9, f32[256,256]{1,0:T(8,128)} %bitcast.10, f32[4,512,256]{2,1,0:T(8,128)} %bitcast.8, f32[4,32,384]{2,1,0:T(8,128)} %bitcast.13, f32[4,32,512]{2,1,0:T(8,128)} %bitcast.11, ...), custom_call_target="tpu_custom_call" | custom-call | tf_op jit(solution)/shard_map/forward_solve/pallas_call | solution.py:480
  68.6 1.6 %copy.15 = f32[1,4,32,384]{3,2,1,0:T(8,128)} copy(f32[1,4,32,384]{3,2,1,0:T(8,128)} %bitcast.12) | data formatting | bytes 393216
  70.2 1.4 %copy.16 = f32[32,384]{1,0:T(8,128)} copy(f32[32,384]{1,0:T(8,128)} %get-tuple-element.9) | data formatting | bytes 98304

commit v2 on v1

--- a/solution.py
+++ b/solution.py
@@ -1,4 +1,5 @@
 import functools
+import math
 
 import jax
 import jax.numpy as jnp
@@ -12,8 +13,10 @@
 NT = (((1,), (1,)), ((), ()))
 HALVES = 2
 LAG = 2
-BEFORE = 1
-SHIFT = (0, 0, 0, 0)
+PLAN = ((0,), (), (1,), (4,), (2, 5, 3, 6, 9, 8))
+SHIFT = (0, 0, 1, 2)
+JOIN = 13
+ROUNDS = (1, 3, 5)
 
 
 def split(a):
@@ -39,6 +42,8 @@
     root_coupling,
     root_rhs,
     root_inverse,
+    sep_final,
+    root_final,
     sep_out,
     root_out,
     v_rhs,
@@ -47,7 +52,8 @@
     v_sep,
     g_inv,
     g_chain,
-    g_rc,
+    g_m,
+    g_q,
     g_rr,
     g_ri,
     part,
@@ -64,9 +70,9 @@
     padded,
     turned,
     pieces,
-    root_send,
-    root_recv,
-    root_full,
+    rr_full,
+    rr_out,
+    root_pieces,
     load,
     own_load,
     w_send,
@@ -85,6 +91,15 @@
     o_recv,
     x_send,
     x_recv,
+    q_send,
+    q_recv,
+    m_send,
+    m_recv,
+    qz_send,
+    qz_recv,
+    r_send,
+    r_recv,
+    end,
 ):
     seps, rows, right = v_sep.shape
     width = v_coup.shape[1]
@@ -105,6 +120,7 @@
     y_peer = at(z, 1 - y, c)
     far_peer = at(z, 1 - y, 1 - c)
     x_peer = (1 - layer, me)
+    lanes = width // 4
     left, right_peer = (layer, me - 4), (layer, me + 4)
     z_peers = [at((z + d) % n_z, y, c) for d in range(1, n_z)]
     plane_peers = [core_peer, y_peer, far_peer]
@@ -115,16 +131,28 @@
         )
 
     barrier = pltpu.get_barrier_semaphore()
-    peers = plane_peers + z_peers + [x_peer]
-    for peer in peers:
+    near = plane_peers + [x_peer]
+    for peer in near:
         pl.semaphore_signal(barrier, inc=1, device_id=peer, device_id_type=MESH)
+
+    @pl.when(z > 0)
+    def _():
+        pl.semaphore_signal(barrier, inc=1, device_id=left, device_id_type=MESH)
+
+    @pl.when(z < n_z - 1)
+    def _():
+        pl.semaphore_signal(barrier, inc=1, device_id=right_peer, device_id_type=MESH)
+
+    def enter():
+        pl.semaphore_wait(barrier, len(near) + jnp.minimum(z, 1) + jnp.minimum(n_z - 1 - z, 1))
+
 
     own_rows = pl.ds(pl.multiple_of(plane * rows, rows), rows)
     y_rows = pl.ds(pl.multiple_of((2 * (1 - y) + c) * rows, rows), rows)
     weights = [(sep_inverse.at[k], g_inv.at[k]) for k in range(seps)]
     weights += [(sep_coupling.at[k], g_chain.at[k]) for k in range(last)]
-    weights += [(root_coupling, g_rc), (root_rhs, g_rr), (root_inverse, g_ri)]
-    inv_at, chain_at, rc_at, rr_at, ri_at = 0, seps, seps + last, seps + last + 1, seps + last + 2
+    weights += [(root_rhs, g_rr), (root_inverse, g_ri)]
+    inv_at, chain_at, rr_at, ri_at = 0, seps, seps + last, seps + last + 1
 
     loads = [
         pltpu.make_async_copy(leaf_inverse, v_inv, load.at[0]),
@@ -138,8 +166,59 @@
         pltpu.make_async_copy(source, dest.at[own_rows, :], own_load.at[n])
         for n, (source, dest) in enumerate(weights)
     ]
-    for copy in own_loads:
+    my_lanes = pl.ds(pl.multiple_of(plane * lanes, 128), lanes)
+    q_rows = pl.ds(pl.multiple_of(z * zrows + plane * rows, rows), rows)
+    z_rows = pl.ds(pl.multiple_of(z * zrows, rows), zrows)
+    own_quarter = pltpu.make_async_copy(root_coupling.at[:, my_lanes], g_q.at[q_rows, :], load.at[3 + seps])
+    for copy in own_loads + [own_quarter]:
         copy.start()
+
+    plane_of = (2 * y + 1 - c, 2 * (1 - y) + c, 2 * (1 - y) + 1 - c)
+
+    def quarter_copy(n):
+        there = pl.ds(pl.multiple_of(plane_of[n] * lanes, 128), lanes)
+        return remote(
+            root_coupling.at[:, there], g_q.at[q_rows, :], q_send.at[n], q_recv.at[n], plane_peers[n]
+        )
+
+    def quarter_hop(side, number, sent):
+        owner = (z - number, z + number)[side] if sent else (z - 1 - number, z + 1 + number)[side]
+        block = g_q.at[pl.ds(pl.multiple_of(owner * zrows, rows), zrows), :]
+        return remote(
+            block, block, qz_send.at[side, number], qz_recv.at[side, number], (right_peer, left)[side]
+        )
+
+    def takes(side, number):
+        return (z - 1 - number >= 0, z + 1 + number < n_z)[side]
+
+    def gives(side, number):
+        far = (z - number >= 0, z + number < n_z)[side]
+        return jnp.logical_and(far, (z < n_z - 1, z > 0)[side])
+
+    def quarter_round(number):
+        for side in range(2):
+            if number > 0:
+
+                @pl.when(takes(side, number - 1))
+                def _():
+                    quarter_hop(side, number - 1, False).wait_recv()
+
+            if number < n_z - 1:
+
+                @pl.when(gives(side, number))
+                def _():
+                    quarter_hop(side, number, True).start()
+
+    def product_copy(n):
+        return remote(
+            g_m.at[:, my_lanes], g_m.at[:, my_lanes], m_send.at[n], m_recv.at[n], plane_peers[n]
+        )
+
+    def send_weights(place):
+        for n in PLAN[place]:
+            weight(0, numbers[n]).start()
+
+    numbers = tuple(range(seps + last)) + (None, rr_at, ri_at)
 
     def weight(way, n):
         source, dest = weights[n]
@@ -183,6 +262,10 @@
     loads[1].wait()
     leaf = dot3(split(v_inv[...]), split(v_rhs[...]), NN)
     leaf_t = split(leaf.T)
+
+    share = quarter // 2
+    rr_start = pl.multiple_of(half * c + quarter * y + share * layer, 8)
+    rr_cols = pl.ds(rr_start, share)
 
     def stage_a(k):
         keep = jnp.where(parent[0, 0] <= k, -1.0, 0.0).astype(jnp.float32)
@@ -193,9 +276,10 @@
         padded[own_rows, :] = v_sep[k]
         part[k, :, zlanes] += padded[...].T
         if k == 0:
-            pl.semaphore_wait(barrier, len(peers))
-            for n in range(BEFORE):
-                weight(0, n).start()
+            enter()
+            for n in range(3):
+                quarter_copy(n).start()
+            send_weights(0)
         for q in range(2):
             core_copy(k, q).start()
 
@@ -284,8 +368,7 @@
         return remote(block, block, a_send.at[k, h, d - 1], a_recv.at[k, h, d - 1], z_peers[d - 1])
 
     def out_copy(k, n):
-        peer_plane = (2 * y + 1 - c, 2 * (1 - y) + c, 2 * (1 - y) + 1 - c)[n]
-        rows_there = pl.ds(pl.multiple_of(peer_plane * rows, rows), rows)
+        rows_there = pl.ds(pl.multiple_of(plane_of[n] * rows, rows), rows)
         return remote(
             turned.at[k, rows_there, :], pieces.at[k, n], o_send.at[k, n], o_recv.at[k, n], plane_peers[n]
         )
@@ -298,14 +381,33 @@
     def assemble(k):
         for n in range(3):
             out_copy(k, n).wait_recv()
-        own = turned[k, own_rows, :][:, :quarter]
-        by_core, by_y, by_far = (pieces[k, n][:, :quarter] for n in range(3))
+        found = [turned[k, own_rows, :]] + [pieces[k, n] for n in range(3)]
+        if k == seps:
+            found = [found[n] + root_pieces[n] for n in range(4)]
+        own, by_core, by_y, by_far = (block[:, :quarter] for block in found)
         low_y, low_core = y == 0, c == 0
         same = (jnp.where(low_y, own, by_y), jnp.where(low_y, by_y, own))
         other = (jnp.where(low_y, by_core, by_far), jnp.where(low_y, by_far, by_core))
         blocks = [jnp.where(low_core, same[n], other[n]) for n in range(2)]
         blocks += [jnp.where(low_core, other[n], same[n]) for n in range(2)]
         return jnp.concatenate(blocks, axis=1)
+
+    def join():
+        weight_ready(ri_at)
+        g_m[:, my_lanes] = dot3(split(g_ri[...]), split(g_q[...]), NN)
+        for n in range(3):
+            product_copy(n).start()
+        weight_ready(rr_at)
+        for q in range(2):
+            core_copy(0, q).wait_send()
+        part[0, :, pl.ds(0, zrows)] = g_rr[...].T
+        rr_full[:, zlanes] = part[0, rr_cols, pl.ds(0, zrows)]
+        for d in range(1, n_z):
+            rr_along_z(d, False).start()
+
+    def rr_along_z(d, sender):
+        block = rr_full.at[:, z_lanes((z - d + n_z) % n_z if sender else z)]
+        return remote(block, block, r_send.at[d - 1], r_recv.at[d - 1], z_peers[d - 1])
 
     def wait_along_z(ref, k, h):
         for d in range(1, n_z):
@@ -333,29 +435,33 @@
     stage_a(0)
     stage_a(1)
     stage_b(0)
+    send_weights(1)
     for k in range(2, seps):
         stage_a(k)
         stage_b(k - 1)
+        send_weights(k)
     stage_b(last)
-    order = [inv_at, inv_at + 1]
-    for k in range(1, seps):
-        order += [chain_at + k - 1] + [inv_at + k + 1] * (k < last)
-    order += [rc_at, rr_at, ri_at]
-    for n in order:
-        if n >= BEFORE:
-            weight(0, n).start()
+    send_weights(seps)
+    own_quarter.wait()
+    for n in range(3):
+        quarter_copy(n).wait_recv()
+    quarter_round(0)
+    order = [numbers[n] for place in PLAN for n in place]
     for n in order:
         weight(1, n).start()
     chunks = [(k, h) for k in range(seps) for h in range(HALVES)]
-    end = len(chunks) + LAG * (n_z - 1)
-    relays = {}
-    for i, n in enumerate(order):
-        relays.setdefault(2 if n < BEFORE else len(chunks) - 1 + (2 * (i + 1 - BEFORE) * HALVES) // 6, []).append(n)
+    last_step = len(chunks) + LAG * (n_z - 1)
+    relays, clock = {}, -1 - 2 * len(PLAN[0]) / 3
+    for place, numbered in enumerate(PLAN):
+        for n in numbered:
+            clock += 2 / 3
+            relays.setdefault(max(1, math.ceil(clock)), []).append(numbers[n])
+        clock += HALVES if place < seps else 0
     chains = {}
     for j, (k, h) in enumerate(chunks):
         chains.setdefault(j + LAG * (n_z - 1) + SHIFT[min(k, 3)], []).append((k, h))
 
-    for step in range(max(end, max(chains) + 1)):
+    for step in range(max(last_step, max(chains) + 1, JOIN + 1)):
         for n in relays.pop(step, []):
             relay(n)
         for number in reversed(range(n_z - 1)):
@@ -369,41 +475,54 @@
             finish(*chunks[j])
         for k, h in chains.get(step, []):
             chain(k, h)
+        if step in ROUNDS[: n_z - 1]:
+            quarter_round(1 + ROUNDS.index(step))
+        if step == JOIN:
+            join()
     for step in sorted(relays):
         for n in relays[step]:
             relay(n)
 
-    for n in range(rc_at, ri_at + 1):
-        weight_ready(n)
-    root_rhs_t = g_rr[...].T
-    turned_rr = part.at[0, :, pl.ds(0, zrows)]
-    for k in range(seps):
-        for q in range(2):
-            core_copy(k, q).wait_send()
-    turned_rr[...] = root_rhs_t
-
-    def swap(h):
-        where = pl.ds(h * sub, sub)
-        return remote(root_send.at[where, :], root_recv.at[where, :], x_send.at[h], x_recv.at[h], x_peer)
-
+    for k in range(last):
+        sep_out[k] = assemble(k)
+    for d in range(1, n_z):
+        rr_along_z(d, True).wait_recv()
+    rr_out[...] = jnp.zeros_like(rr_out)
+    rr_out[pl.ds(pl.multiple_of(share * layer, 8), share), :] = dot3(split(rr_full[...]), split(g_ri[...]), NT)
+    for n in range(3):
+        product_copy(n).wait_recv()
+    product = split(g_m[...])
     for h in range(HALVES):
         where = pl.ds(h * sub, sub)
         wait_along_z(solved.at[last], last, h)
-        root_send[where, :] = dot3(split(solved[last, where, :]), split(g_rc[...]), NT)
-        swap(h).start()
-    for k in range(last):
-        sep_out[k] = assemble(k)
-    for h in range(HALVES):
-        where = pl.ds(h * sub, sub)
-        swap(h).wait_recv()
-        my_cols = pl.ds(pl.multiple_of(half * c + quarter * y + h * sub, 8), sub)
-        root_full[where, zlanes] = part[0, my_cols, pl.ds(0, zrows)] - (root_send[where, :] + root_recv[where, :])
-        send_along_z(root_full, seps, h)
+        rr_out[where, :] = rr_out[where, :] - dot3(split(solved[last, where, :]), product, NT)
+
+    others = [(1 - layer, me + p - plane) for p in (plane,) + plane_of]
+
+    def cross_copy(n):
+        rows_there = pl.ds(pl.multiple_of(((plane,) + plane_of)[n] * rows, rows), rows)
+        return remote(
+            turned.at[seps, rows_there, :], root_pieces.at[n], x_send.at[n], x_recv.at[n], others[n]
+        )
+
+    turned[seps, :, pl.ds(0, quarter)] = rr_out[...].T
+    for n in (3, 2, 1, 0):
+        cross_copy(n).start()
+    for n in range(3):
+        out_copy(seps, n).start()
     sep_out[last] = assemble(last)
-    for h in range(HALVES):
-        wait_along_z(root_full, seps, h)
-    turn(seps, dot3(split(root_full[...]), split(g_ri[...]), NT))
+    for n in range(4):
+        cross_copy(n).wait_recv()
     root_out[...] = assemble(seps)
+    for k in range(1, seps):
+        for q in range(2):
+            core_copy(k, q).wait_send()
+    ends = [
+        pltpu.make_async_copy(sep_out, sep_final, end.at[0]),
+        pltpu.make_async_copy(root_out, root_final, end.at[1]),
+    ]
+    for copy in ends:
+        copy.start()
 
     for way in range(3):
         for n in range(len(weights)):
@@ -419,15 +538,33 @@
         def _():
             bwd_copy(k, h).wait_send()
 
-    for k in range(seps + 1):
-        ref = solved.at[k] if k < seps else root_full
+    for k in range(seps):
         for h in range(HALVES):
             for d in range(1, n_z):
-                along_z(ref, k, h, d, False).wait_send()
+                along_z(solved.at[k], k, h, d, False).wait_send()
+    for k in range(seps + 1):
         for n in range(3):
             out_copy(k, n).wait_send()
-    for h in range(HALVES):
-        swap(h).wait_send()
+    for n in range(4):
+        cross_copy(n).wait_send()
+    for n in range(3):
+        quarter_copy(n).wait_send()
+        product_copy(n).wait_send()
+    for d in range(1, n_z):
+        rr_along_z(d, False).wait_send()
+    for number in range(n_z - 1):
+        for side in range(2):
+
+            @pl.when(gives(side, number))
+            def _():
+                quarter_hop(side, number, True).wait_send()
+
+    for copy in ends:
+        copy.wait()
+
+
+def keep_out(a):
+    return pltpu.with_memory_space_constraint(a, pltpu.HBM)
 
 
 def fused(
@@ -450,8 +587,10 @@
     f32 = jnp.float32
     dma = pltpu.SemaphoreType.DMA
     vmem = pl.BlockSpec(memory_space=pltpu.VMEM)
-    hbm = pl.BlockSpec(memory_space=pl.ANY)
+    hbm = pl.BlockSpec(memory_space=pltpu.HBM)
     scratch = [
+        (seps, rows, right),
+        (rows, right),
         (deep, right),
         (deep, deep),
         (seps, width, deep),
@@ -459,6 +598,7 @@
         (seps, zrows, width),
         (seps - 1, zrows, width),
         (zrows, width),
+        (width, width // 4),
         (zrows, right),
         (zrows, width),
         (seps, right, width),
@@ -469,14 +609,15 @@
         (zrows, right),
         (seps + 1, zrows, 128),
         (seps + 1, 3, rows, 128),
+        (quarter // 2, width),
         (quarter, zrows),
-        (quarter, zrows),
-        (quarter, width),
+        (4, rows, 128),
     ]
-    n_w = 2 * seps + 2
-    sems = [(3 + seps,), (n_w,)]
+    n_w = 2 * seps + 1
+    sems = [(4 + seps,), (n_w,)]
     sems += [(3, n_w)] * 2 + [(seps, 2)] * 2 + [(seps, HALVES)] * 6
-    sems += [(seps + 1, HALVES, n_z - 1)] * 2 + [(seps + 1, 3)] * 2 + [(HALVES,)] * 2
+    sems += [(seps, HALVES, n_z - 1)] * 2 + [(seps + 1, 3)] * 2 + [(4,)] * 2
+    sems += [(3,)] * 4 + [(2, n_z - 1)] * 2 + [(n_z - 1,)] * 2 + [(2,)]
     sep, root = pl.pallas_call(
         functools.partial(kernel, n_z),
         out_shape=(
@@ -484,14 +625,15 @@
             jax.ShapeDtypeStruct((rows, right), f32),
         ),
         in_specs=[pl.BlockSpec(memory_space=pltpu.SMEM)] + [hbm] * 9,
-        out_specs=(vmem, vmem),
+        out_specs=(pl.BlockSpec(memory_space=pl.ANY),) * 2,
         scratch_shapes=[pltpu.VMEM(s, f32) for s in scratch] + [dma(s) for s in sems],
         compiler_params=pltpu.CompilerParams(
-            collective_id=0, has_side_effects=True, vmem_limit_bytes=60 * 2**20
+            collective_id=0, has_side_effects=True, vmem_limit_bytes=24 * 2**20
         ),
         name="forward_solve",
     )(
         parent,
+        *map(keep_out, (
         leaf_rhs.reshape(leaf_rhs.shape[2:]),
         leaf_inverse.reshape(leaf_inverse.shape[2:]),
         leaf_coupling.reshape(leaf_coupling.shape[2:]),
@@ -501,7 +643,27 @@
         root_coupling.reshape(root_coupling.shape[1:]),
         root_rhs,
         root_inverse,
+        )),
     )
+    return write_out(sep, root)
+
+
+def write(sep, root, sep_out, root_out):
+    sep_out[...] = sep[...]
+    root_out[...] = root[...]
+
+
+def write_out(sep, root):
+    vmem = pl.BlockSpec(memory_space=pltpu.VMEM)
+    shapes = tuple(jax.ShapeDtypeStruct(a.shape, a.dtype) for a in (sep, root))
+    sep, root = pl.pallas_call(
+        write,
+        out_shape=shapes,
+        in_specs=[vmem, vmem],
+        out_specs=(vmem, vmem),
+        compiler_params=pltpu.CompilerParams(vmem_limit_bytes=2 * 2**20),
+        name="write_out",
+    )(sep, root)
     return sep[None], root
 
 
@@ -563,10 +725,12 @@
         fits = (
             n_layer == 2
             and n_row in (8, 16)
+            and width % 512 == 0
             and width % (128 * n_z) == 0
             and right % (32 * HALVES) == 0
+            and right % 64 == 0
             and right // 4 <= 128
-            and arrays[4].shape[1] >= 3
+            and arrays[4].shape[1] == 4
         )
         return functools.partial(fused, n_z)(*arrays) if fits else body(*arrays)
 

time: 71.8 us -> 65.4 us (0.911)
  Pallas kernels: 67.3 us -> 64 us
  local copies, waits for them, and re-layouts: 3.04 us -> 0 us
    pallas_call x1, Pallas kernels: 67.3 us -> 63.3 us  [fused(): pl.pallas_call(functools.partial(kernel, n_z), out_shape=(jax.ShapeDtypeS...]
    unnamed x2 -> x0, local copies, waits for them, and re-layouts: 3.04 us -> none
where the time goes in v2:
time: 65.4 us; the launch traced here: 65.3 us
  Pallas kernels  64 us (98%)
  between operations  1.29 us (2%)
    pallas_call x1, Pallas kernels, fused(): pl.pallas_call(functools.partial(kernel, n_z), out_shape=(jax.ShapeDtypeS...  63.3 us

profile of v2, /device:TPU:0, one launch (start us, length us, event | category | flops | bytes accessed | tf_op | source)
XLA Modules:
  0.0 65.3 jit_solution(5837921018441527239)
XLA Ops:
  1.3 63.3 %forward_solve.1 = (f32[4,32,384]{2,1,0:T(8,128)S(1)}, f32[32,384]{1,0:T(8,128)S(1)}) custom-call(s32[1,1]{1,0:T(1,128)S(6)} %copy.12.parent, f32[256,384]{1,0:T(8,128)} %bitcast.9, f32[256,256]{1,0:T(8,128)} %bitcast.10, f32[4,512,256]{2,1,0:T(8,128)} %bitcast.8, f32[4,32,384]{2,1,0:T(8,128)} %bitcast.12, f32[4,32,512]{2,1,0:T(8,128)} %bitcast.11, ...), custom_call_target="tpu_custom_call" | custom-call | tf_op jit(solution)/shard_map/forward_solve/pallas_call | solution.py:621
  64.6 0.7 %write_out.1 = (f32[4,32,384]{2,1,0:T(8,128)}, f32[32,384]{1,0:T(8,128)}) custom-call(f32[4,32,384]{2,1,0:T(8,128)S(1)} %get-tuple-element.6.sep, f32[32,384]{1,0:T(8,128)S(1)} %get-tuple-element.7.root), custom_call_target="tpu_custom_call" | custom-call | tf_op jit(solution)/shard_map/write_out/pallas_call | solution.py:659

commit v3 on v2

--- a/solution.py
+++ b/solution.py
@@ -14,8 +14,8 @@
 HALVES = 2
 LAG = 2
 PLAN = ((0,), (), (1,), (4,), (2, 5, 3, 6, 9, 8))
-SHIFT = (0, 0, 1, 2)
-JOIN = 13
+SHIFT = (0, 0, 1, 3)
+JOIN = 12
 ROUNDS = (1, 3, 5)
 
 
@@ -234,11 +234,16 @@
             y_peer if way == 0 else core_peer,
         )
 
+    relayed = set()
+
     def relay(n):
-        weight(0, n).wait_recv()
-        weight(2, n).start()
+        if n not in relayed:
+            relayed.add(n)
+            weight(0, n).wait_recv()
+            weight(2, n).start()
 
     def weight_ready(n):
+        relay(n)
         own_loads[n].wait()
         weight(1, n).wait_recv()
         weight(2, n).wait_recv()
@@ -414,8 +419,12 @@
             along_z(ref, k, h, d, True).wait_recv()
 
     def send_along_z(ref, k, h):
-        for d in range(1, n_z):
-            along_z(ref, k, h, d, False).start()
+        for at_z in range(n_z):
+
+            @pl.when(z == at_z)
+            def _():
+                for d in sorted(range(1, n_z), key=lambda d: -abs((at_z + d) % n_z - at_z)):
+                    along_z(ref, k, h, d, False).start()
 
     def chain(k, h):
         where = pl.ds(h * sub, sub)
@@ -451,10 +460,10 @@
         weight(1, n).start()
     chunks = [(k, h) for k in range(seps) for h in range(HALVES)]
     last_step = len(chunks) + LAG * (n_z - 1)
-    relays, clock = {}, -1 - 2 * len(PLAN[0]) / 3
+    relays, clock = {}, -1 - HALVES * len(PLAN[0]) / 3
     for place, numbered in enumerate(PLAN):
         for n in numbered:
-            clock += 2 / 3
+            clock += HALVES / 3
             relays.setdefault(max(1, math.ceil(clock)), []).append(numbers[n])
         clock += HALVES if place < seps else 0
     chains = {}

time: 65.4 us -> 64.6 us (0.988)
  Pallas kernels: 64 us -> 63.2 us
    pallas_call x1, Pallas kernels: 63.3 us -> 62.5 us  [fused(): pl.pallas_call(functools.partial(kernel, n_z), out_shape=(jax.ShapeDtypeS...]
where the time goes in v3:
time: 64.6 us; the launch traced here: 64.5 us
  Pallas kernels  63.2 us (98%)
  between operations  1.29 us (2%)
    pallas_call x1, Pallas kernels, fused(): pl.pallas_call(functools.partial(kernel, n_z), out_shape=(jax.ShapeDtypeS...  62.5 us

profile of v3, /device:TPU:0, one launch (start us, length us, event | category | flops | bytes accessed | tf_op | source)
XLA Modules:
  0.0 64.5 jit_solution(15530214378570445509)
XLA Ops:
  1.3 62.5 %forward_solve.1 = (f32[4,32,384]{2,1,0:T(8,128)S(1)}, f32[32,384]{1,0:T(8,128)S(1)}) custom-call(s32[1,1]{1,0:T(1,128)S(6)} %copy.12.parent, f32[256,384]{1,0:T(8,128)} %bitcast.9, f32[256,256]{1,0:T(8,128)} %bitcast.10, f32[4,512,256]{2,1,0:T(8,128)} %bitcast.8, f32[4,32,384]{2,1,0:T(8,128)} %bitcast.12, f32[4,32,512]{2,1,0:T(8,128)} %bitcast.11, ...), custom_call_target="tpu_custom_call" | custom-call | tf_op jit(solution)/shard_map/forward_solve/pallas_call | solution.py:630
  63.8 0.7 %write_out.1 = (f32[4,32,384]{2,1,0:T(8,128)}, f32[32,384]{1,0:T(8,128)}) custom-call(f32[4,32,384]{2,1,0:T(8,128)S(1)} %get-tuple-element.6.sep, f32[32,384]{1,0:T(8,128)S(1)} %get-tuple-element.7.root), custom_call_target="tpu_custom_call" | custom-call | tf_op jit(solution)/shard_map/write_out/pallas_call | solution.py:668

commit v4 on v3

--- a/solution.py
+++ b/solution.py
@@ -14,7 +14,7 @@
 HALVES = 2
 LAG = 2
 PLAN = ((0,), (), (1,), (4,), (2, 5, 3, 6, 9, 8))
-SHIFT = (0, 0, 1, 3)
+SHIFT = (0, 0, 1, 2)
 JOIN = 12
 ROUNDS = (1, 3, 5)
 
@@ -494,6 +494,8 @@
 
     for k in range(last):
         sep_out[k] = assemble(k)
+    early = pltpu.make_async_copy(sep_out.at[pl.ds(0, last)], sep_final.at[pl.ds(0, last)], end.at[2])
+    early.start()
     for d in range(1, n_z):
         rr_along_z(d, True).wait_recv()
     rr_out[...] = jnp.zeros_like(rr_out)
@@ -527,7 +529,7 @@
         for q in range(2):
             core_copy(k, q).wait_send()
     ends = [
-        pltpu.make_async_copy(sep_out, sep_final, end.at[0]),
+        pltpu.make_async_copy(sep_out.at[last], sep_final.at[last], end.at[0]),
         pltpu.make_async_copy(root_out, root_final, end.at[1]),
     ]
     for copy in ends:
@@ -568,7 +570,7 @@
             def _():
                 quarter_hop(side, number, True).wait_send()
 
-    for copy in ends:
+    for copy in ends + [early]:
         copy.wait()
 
 
@@ -626,7 +628,7 @@
     sems = [(4 + seps,), (n_w,)]
     sems += [(3, n_w)] * 2 + [(seps, 2)] * 2 + [(seps, HALVES)] * 6
     sems += [(seps, HALVES, n_z - 1)] * 2 + [(seps + 1, 3)] * 2 + [(4,)] * 2
-    sems += [(3,)] * 4 + [(2, n_z - 1)] * 2 + [(n_z - 1,)] * 2 + [(2,)]
+    sems += [(3,)] * 4 + [(2, n_z - 1)] * 2 + [(n_z - 1,)] * 2 + [(3,)]
     sep, root = pl.pallas_call(
         functools.partial(kernel, n_z),
         out_shape=(

time: 64.6 us -> 64.4 us (level)
  no operation moved by 1% of the time
where the time goes in v4:
time: 64.4 us; the launch traced here: 64.3 us
  Pallas kernels  63 us (98%)
  between operations  1.29 us (2%)
    pallas_call x1, Pallas kernels, fused(): pl.pallas_call(functools.partial(kernel, n_z), out_shape=(jax.ShapeDtypeS...  62.3 us

profile of v4, /device:TPU:0, one launch (start us, length us, event | category | flops | bytes accessed | tf_op | source)
XLA Modules:
  0.0 64.3 jit_solution(8554003766293568831)
XLA Ops:
  1.3 62.3 %forward_solve.1 = (f32[4,32,384]{2,1,0:T(8,128)S(1)}, f32[32,384]{1,0:T(8,128)S(1)}) custom-call(s32[1,1]{1,0:T(1,128)S(6)} %copy.12.parent, f32[256,384]{1,0:T(8,128)} %bitcast.9, f32[256,256]{1,0:T(8,128)} %bitcast.10, f32[4,512,256]{2,1,0:T(8,128)} %bitcast.8, f32[4,32,384]{2,1,0:T(8,128)} %bitcast.12, f32[4,32,512]{2,1,0:T(8,128)} %bitcast.11, ...), custom_call_target="tpu_custom_call" | custom-call | tf_op jit(solution)/shard_map/forward_solve/pallas_call | solution.py:632
  63.6 0.7 %write_out.1 = (f32[4,32,384]{2,1,0:T(8,128)}, f32[32,384]{1,0:T(8,128)}) custom-call(f32[4,32,384]{2,1,0:T(8,128)S(1)} %get-tuple-element.6.sep, f32[32,384]{1,0:T(8,128)S(1)} %get-tuple-element.7.root), custom_call_target="tpu_custom_call" | custom-call | tf_op jit(solution)/shard_map/write_out/pallas_call | solution.py:670
